TPU v7x, 32 devices: a whole 2x2x4 slice. The times are simulated.
32 devices in a mesh: aa: 8 (over z, y), ba: 4 (over x, core).
Axes of the slice: x: 2, y: 2, z: 4, core: 2. Of those that a mesh axis runs over, the one named last changes fastest.
Arguments:
- table_a: bfloat16 [6144, 128], P(('aa', 'ba')), may hold values from -40 to 40
- table_b: bfloat16 [4096, 128], P(('aa', 'ba')), may hold values from -40 to 40
- index_a: int32 [1536], P(('aa', 'ba')), may hold values from 0 to 191
- index_b: int32 [1024], P(('aa', 'ba')), may hold values from 0 to 127
- rotation_prev: bfloat16 [128, 128], replicated, may hold values from -0.5 to 0.5
- column_prior: bfloat16 [1024], P(('aa', 'ba')), may hold values from -8 to 8
Outputs:
- rotation: float32 [128, 128], replicated
- potential_a: float32 [1536], P(('aa', 'ba'))
- potential_b: float32 [1024], P(('aa', 'ba'))
Inputs may be any that keep to these rules, and one draw needn't show every extreme that they name: `index_a`: entry r is a node of the block of 192 table rows that starts at row (r // 48) * 192, counted from that block's start. `index_b`: entry r is a node of the block of 128 table rows that starts at row (r // 32) * 128, counted from that block's start.
All inputs are finite; a program needn't handle non-finite values.
Results may differ from a plain program's by a relative error of at most 0.0003.
Values may be sent and summed in bfloat16 or wider, within the bound.
A program may use at most 64 MiB of HBM per device.

v0:
```python
import math

import jax
import jax.numpy as jnp
from jax import lax
from jax.sharding import PartitionSpec as P

PASSES = 3
NS_ITERS = 8


SCORE_SCALE = 0.0625


def combined_all(x, axis, combine):
    everything = jax.tree.map(lambda part: lax.all_gather(part, axis), x)
    initial = jax.tree.map(lambda part: part[0], everything)

    def hop(k, so_far):
        return combine(so_far, jax.tree.map(lambda part: part[k], everything))

    return lax.fori_loop(1, lax.axis_size(axis), hop, initial)


def polar_factor(covariance):
    current = covariance / jnp.sqrt(jnp.sum(covariance * covariance) + 1e-06)
    for sweep in range(NS_ITERS):
        square = jnp.dot(current, current.T, precision=lax.Precision.HIGHEST)
        current = 1.5 * current - 0.5 * jnp.dot(square, current, precision=lax.Precision.HIGHEST)
    return current


def combine_totals(first, second):
    peak = jnp.maximum(first[0], second[0])
    return (peak, first[1] * jnp.exp(first[0] - peak) + second[1] * jnp.exp(second[0] - peak))


def row_totals(logits):
    local_peak = jnp.max(logits, axis=1)
    local_mass = jnp.sum(jnp.exp(logits - local_peak[:, None]), axis=1)
    peak, mass = combined_all((local_peak, local_mass), "ba", combine_totals)
    return (peak, mass)


def column_totals(logits):
    local_peak = jnp.max(logits, axis=0)
    local_mass = jnp.sum(jnp.exp(logits - local_peak[None, :]), axis=0)
    peak, mass = combined_all((local_peak, local_mass), "aa", combine_totals)
    return (peak, mass)


def local(table_a, table_b, index_a, index_b, rotation_prev, column_prior):
    own_a = jnp.take(table_a, index_a, axis=0)
    own_b = jnp.take(table_b, index_b, axis=0)
    rows_a = lax.all_gather(own_a, "ba", axis=0, tiled=True)
    rows_b, prior_low = (
        lax.all_gather(own_b, "aa", axis=0, tiled=True),
        lax.all_gather(column_prior, "aa", axis=0, tiled=True),
    )
    prior = prior_low.astype(jnp.float32)
    devices_all = lax.axis_size("aa") * lax.axis_size("ba")
    total_a = own_a.shape[0] * devices_all
    total_b = own_b.shape[0] * devices_all
    float_a = rows_a.astype(jnp.float32)
    float_b = rows_b.astype(jnp.float32)
    turned_prev = jnp.dot(rows_b, rotation_prev.T, preferred_element_type=jnp.float32)
    logits = (
        jnp.dot(float_a, turned_prev.T, precision=lax.Precision.HIGHEST) * SCORE_SCALE
        + prior[None, :]
    )
    peak, mass = row_totals(logits)
    weights = jnp.exp(logits - peak[:, None]) / mass[:, None]
    mixed = jnp.dot(weights, float_b, precision=lax.Precision.HIGHEST)
    partial_sum = jnp.dot(float_a.T, mixed, precision=lax.Precision.HIGHEST)
    covariance = lax.psum(partial_sum, ("aa", "ba")) / total_a
    rotation = polar_factor(covariance)
    turned = jnp.dot(float_b, rotation.T, precision=lax.Precision.HIGHEST)
    scores = jnp.dot(float_a, turned.T, precision=lax.Precision.HIGHEST) * SCORE_SCALE
    potential_b = prior
    potential_a = jnp.zeros((rows_a.shape[0],), jnp.float32)
    for sweep in range(PASSES):
        peak, mass = row_totals(scores + potential_b[None, :])
        potential_a = -math.log(total_a) - (peak + jnp.log(mass))
        peak, mass = column_totals(scores + potential_a[:, None])
        potential_b = -math.log(total_b) - (peak + jnp.log(mass))
    start_a = lax.axis_index("ba") * own_a.shape[0]
    start_b = lax.axis_index("aa") * own_b.shape[0]
    return (
        rotation,
        lax.dynamic_slice_in_dim(potential_a, start_a, own_a.shape[0]),
        lax.dynamic_slice_in_dim(potential_b, start_b, own_b.shape[0]),
    )


def solution(mesh):
    return jax.shard_map(
        local,
        mesh=mesh,
        in_specs=(
            P(("aa", "ba"), None),
            P(("aa", "ba"), None),
            P(("aa", "ba")),
            P(("aa", "ba")),
            P(),
            P(("aa", "ba")),
        ),
        out_specs=(P(), P(("aa", "ba")), P(("aa", "ba"))),
        check_vma=False,
    )
```

profile of v0, /device:TPU:0, one launch (start us, length us, event | category | flops | bytes accessed | tf_op | source)
XLA Modules:
  0.0 350.4 jit_solution(10896727446416801769)
XLA Ops:
  7.3 0.7 compare_select_fusion
  7.9 0.7 compare_and_fusion
  8.6 0.7 compare_select_fusion.1
  9.2 0.7 compare_and_fusion.1
  9.9 0.6 dynamic-slice
  11.1 0.9 dynamic-update-slice
  12.0 23.1 %all-reduce = bf16[256]{0:T(256)(128)(2,1)S(1)} all-reduce(bf16[256]{0:T(256)(128)(2,1)S(1)} %dynamic-update-slice), channel_id=1, replica_groups=mesh['aa'=8,'ba'=4] {'aa'}, use_global_device_ids=true, to_apply=%add | all-reduce | flops 256 | bytes 1024
  35.2 0.6 gather_fusion.1
  35.8 30.5 %all_gather.94 = bf16[256,128]{1,0:T(8,128)(2,1)S(1)} all-gather(bf16[32,128]{1,0:T(8,128)(2,1)S(1)} %broadcast_select_fusion.1), channel_id=1, replica_groups=mesh['aa'=8,'ba'=4] {'aa'}, dimensions={0}, use_global_device_ids=true | all-gather | bytes 73728 | tf_op jit(solution)/shard_map/all_gather | solution.py:57
  66.4 0.6 gather_fusion
  67.1 5.4 %all_gather.93 = bf16[192,128]{1,0:T(8,128)(2,1)S(1)} all-gather(bf16[48,128]{1,0:T(8,128)(2,1)S(1)} %broadcast_select_fusion), channel_id=1, replica_groups=mesh['aa'=8,'ba'=4] {'ba'}, dimensions={0}, use_global_device_ids=true | all-gather | bytes 61440 | tf_op jit(solution)/shard_map/all_gather | solution.py:55
  74.9 7.2 %all-reduce.12 = (f32[768]{0:T(1024)S(1)}, f32[768]{0:T(1024)S(1)}) all-reduce(f32[768]{0:T(1024)S(1)} %dynamic-update-slice.1, f32[768]{0:T(1024)S(1)} %dynamic-update-slice.2), channel_id=2, replica_groups=mesh['aa'=8,'ba'=4] {'ba'}, use_global_device_ids=true, to_apply=%add.1 | all-reduce | flops 1536 | bytes 12288
  82.7 0.9 fusion.20
  83.6 115.8 %all-reduce.15.cloned.1.call-done = f32[128,128]{1,0:T(8,128)} async-done(((f32[128,128]{1,0:T(8,128)}), f32[128,128]{1,0:T(8,128)}) %all-reduce.15.cloned.1.call-update) | async-done | bytes 65552 | tf_op jit(solution)/shard_map/psum | solution.py:75
  199.5 1.5 multiply_reduce_fusion
  207.2 8.5 %all-reduce.11 = (f32[768]{0:T(1024)S(1)}, f32[768]{0:T(1024)S(1)}) all-reduce(f32[768]{0:T(1024)S(1)} %dynamic-update-slice.3, f32[768]{0:T(1024)S(1)} %dynamic-update-slice.4), channel_id=4, replica_groups=mesh['aa'=8,'ba'=4] {'ba'}, use_global_device_ids=true, to_apply=%add.3 | all-reduce | flops 1536 | bytes 12288
  216.3 19.5 %all-gather.15 = f32[8,1,256]{2,1,0:T(1,128)S(1)} all-gather(f32[1,1,256]{2,1,0:T(1,128)S(1)} %bitcast.143), channel_id=7, replica_groups=mesh['aa'=8,'ba'=4] {'aa'}, dimensions={0}, use_global_device_ids=true | all-gather | bytes 9216 | tf_op jit(solution)/shard_map/all_gather | solution.py:16
  235.8 0.6 copy-done.4
  236.4 16.3 %all-gather.14 = f32[8,1,256]{2,1,0:T(1,128)S(1)} all-gather(f32[1,1,256]{2,1,0:T(1,128)S(1)} %bitcast.140), channel_id=6, replica_groups=mesh['aa'=8,'ba'=4] {'aa'}, dimensions={0}, use_global_device_ids=true | all-gather | bytes 9216 | tf_op jit(solution)/shard_map/all_gather | solution.py:16
  253.3 0.7 slice-done.3
  255.1 5.9 %all-reduce.10 = (f32[768]{0:T(1024)S(1)}, f32[768]{0:T(1024)S(1)}) all-reduce(f32[768]{0:T(1024)S(1)} %dynamic-update-slice.5, f32[768]{0:T(1024)S(1)} %dynamic-update-slice.6), channel_id=8, replica_groups=mesh['aa'=8,'ba'=4] {'ba'}, use_global_device_ids=true, to_apply=%add.5 | all-reduce | flops 1536 | bytes 12288
  261.6 18.3 %all-gather.17 = f32[8,1,256]{2,1,0:T(1,128)S(1)} all-gather(f32[1,1,256]{2,1,0:T(1,128)S(1)} %bitcast.144), channel_id=11, replica_groups=mesh['aa'=8,'ba'=4] {'aa'}, dimensions={0}, use_global_device_ids=true | all-gather | bytes 9216 | tf_op jit(solution)/shard_map/all_gather | solution.py:16
  279.9 0.6 copy-done.5
  280.5 16.3 %all-gather.16 = f32[8,1,256]{2,1,0:T(1,128)S(1)} all-gather(f32[1,1,256]{2,1,0:T(1,128)S(1)} %bitcast.141), channel_id=10, replica_groups=mesh['aa'=8,'ba'=4] {'aa'}, dimensions={0}, use_global_device_ids=true | all-gather | bytes 9216 | tf_op jit(solution)/shard_map/all_gather | solution.py:16
  297.4 0.7 slice-done.4
  299.2 5.8 %all-reduce.9 = (f32[768]{0:T(1024)S(1)}, f32[768]{0:T(1024)S(1)}) all-reduce(f32[768]{0:T(1024)S(1)} %dynamic-update-slice.7, f32[768]{0:T(1024)S(1)} %dynamic-update-slice.8), channel_id=12, replica_groups=mesh['aa'=8,'ba'=4] {'ba'}, use_global_device_ids=true, to_apply=%add.7 | all-reduce | flops 1536 | bytes 12288
  305.6 18.3 %all-gather.19 = f32[8,1,256]{2,1,0:T(1,128)S(1)} all-gather(f32[1,1,256]{2,1,0:T(1,128)S(1)} %bitcast.145), channel_id=15, replica_groups=mesh['aa'=8,'ba'=4] {'aa'}, dimensions={0}, use_global_device_ids=true | all-gather | bytes 9216 | tf_op jit(solution)/shard_map/all_gather | solution.py:16
  323.9 0.6 copy-done.6
  324.5 16.3 %all-gather.18 = f32[8,1,256]{2,1,0:T(1,128)S(1)} all-gather(f32[1,1,256]{2,1,0:T(1,128)S(1)} %bitcast.142), channel_id=14, replica_groups=mesh['aa'=8,'ba'=4] {'aa'}, dimensions={0}, use_global_device_ids=true | all-gather | bytes 9216 | tf_op jit(solution)/shard_map/all_gather | solution.py:16
  341.4 0.7 slice-done.5
  342.4 0.6 dynamic_slice.146
  343.0 0.6 dynamic_slice.147
  (191 shorter events, 15.1 us)
Async XLA Ops:
  7.2 59.2 %copy-start = (bf16[192,128]{1,0:T(8,128)(2,1)S(1)}, bf16[192,128]{1,0:T(8,128)(2,1)}, u32[]{:S(2)}) copy-start(bf16[192,128]{1,0:T(8,128)(2,1)} %param.20) | copy-start | bytes 147460
  7.2 2.7 copy-start.12
  7.2 28.0 %copy-start.2 = (bf16[128,128]{1,0:T(8,128)(2,1)S(1)}, bf16[128,128]{1,0:T(8,128)(2,1)}, u32[]{:S(2)}) copy-start(bf16[128,128]{1,0:T(8,128)(2,1)} %param.21) | copy-start | bytes 98308
  7.2 192.3 %all-reduce.15.cloned.1.call-start = ((), (), s32[]{:S(2)}) async-start(), calls=%async_computation | async-start | bytes 131072 | tf_op jit(solution)/shard_map/psum | solution.py:75
  67.1 5.4 %copy-start.11 = (u32[32]{0:T(128)S(1)}, u32[32]{0:T(128)}, u32[]{:S(2)}) copy-start(u32[32]{0:T(128)} %constant.320) | copy-start | bytes 388
  67.1 5.9 %copy-start.10 = (bf16[128,128]{1,0:T(8,128)(2,1)S(1)}, bf16[128,128]{1,0:T(8,128)(2,1)}, u32[]{:S(2)}) copy-start(bf16[128,128]{1,0:T(8,128)(2,1)} %param.24) | copy-start | bytes 98308
  199.5 2.2 copy-start.3
  205.6 0.6 copy-start.1
  235.8 0.6 copy-start.4
  252.7 0.6 copy-start.7
  253.3 0.7 slice-start.3
  253.3 0.7 slice-start
  279.9 0.6 copy-start.5
  296.8 0.6 copy-start.8
  297.4 0.7 slice-start.4
  297.4 0.7 slice-start.1
  323.9 0.6 copy-start.6
  340.8 0.6 copy-start.9
  341.4 0.7 slice-start.5
  341.4 0.7 slice-start.2
Sparse Core Ops, SparseCore 0:
  83.7 115.6 all-reduce.14
where the time goes:
time: 351 us; the launch traced here: 350 us
  blocking collectives  191 us (54%)
  waiting for transfers between devices  116 us (33%)
  between operations  16.4 us (5%)
  local copies, waits for them, and re-layouts  13.2 us (4%)
  other arithmetic  6.81 us (2%)
  matrix products  6.11 us (2%)
    psum x1, waiting for transfers between devices, local(): covariance = lax.psum(partial_sum, ('aa', 'ba')) / total_a  116 us
    all_gather x6, blocking collectives, combined_all(): everything = jax.tree.map(lambda part: lax.all_gather(part, axis), x)  105 us
    unnamed x5, blocking collectives  50.6 us
    all_gather x1, blocking collectives, local(): lax.all_gather(own_b, 'aa', axis=0, tiled=True)  30.5 us
    unnamed x52, local copies, waits for them, and re-layouts  7.83 us
  transfers between devices with their start and end apart: 1, of which 1 were waited for; matrix products, arithmetic and copies ran while one was open for 0% of the time, Pallas kernels for 0%

commit v1 on v0

--- a/solution.py
+++ b/solution.py
@@ -1,8 +1,11 @@
+import functools
 import math
 
 import jax
 import jax.numpy as jnp
 from jax import lax
+from jax.experimental import pallas as pl
+from jax.experimental.pallas import tpu as pltpu
 from jax.sharding import PartitionSpec as P
 
 PASSES = 3
@@ -49,7 +52,7 @@
     return (peak, mass)
 
 
-def local(table_a, table_b, index_a, index_b, rotation_prev, column_prior):
+def local_collectives(table_a, table_b, index_a, index_b, rotation_prev, column_prior):
     own_a = jnp.take(table_a, index_a, axis=0)
     own_b = jnp.take(table_b, index_b, axis=0)
     rows_a = lax.all_gather(own_a, "ba", axis=0, tiled=True)
@@ -92,6 +95,321 @@
     )
 
 
+LANES = 128
+PACK = 16
+LOG2E = math.log2(math.e)
+LN2 = math.log(2.0)
+MESH = pl.DeviceIdType.MESH
+SCORE_BYTES = 8 * 2**20
+NT = (((1,), (1,)), ((), ()))
+TN = (((0,), (0,)), ((), ()))
+
+
+def mm(x, y, dims=(((1,), (0,)), ((), ()))):
+    return lax.dot_general(x, y, dims, preferred_element_type=jnp.float32)
+
+
+def pieces(x, count):
+    terms = []
+    for k in range(count):
+        term = x.astype(jnp.bfloat16)
+        terms.append(term)
+        if k + 1 < count:
+            x = x - term.astype(jnp.float32)
+    return terms
+
+
+def square_product(left, right, dims_right):
+    l0, l1 = pieces(left, 2)
+    r0, r1 = pieces(right, 2)
+    lhs = jnp.concatenate([l0, l1], axis=1)
+    if dims_right == 1:
+        rhs = jnp.concatenate(
+            [jnp.concatenate([r0, r0], axis=1), jnp.concatenate([r1, r1], axis=1)], axis=0
+        )
+        out = mm(lhs, rhs, NT)
+    else:
+        rhs = jnp.concatenate(
+            [jnp.concatenate([r0, r1], axis=1), jnp.concatenate([r0, r1], axis=1)], axis=0
+        )
+        out = mm(lhs, rhs)
+    n = left.shape[0]
+    return out[:, :n] + out[:, n:]
+
+
+def log2(x):
+    return jnp.log(x) * LOG2E
+
+
+def kernel(na, nb, ad, bd,
+           ta_ref, tb_ref, ia_ref, ib_ref, rot_ref, prior_ref,
+           rot_out, pa_out, pb_out,
+           a_buf, b_buf, s_buf, w_buf, cov_buf, cov2_buf, lse_buf, pa_buf, pb_buf,
+           az_s, az_r, bz_s, bz_r, ay_s, ay_r, by_s, by_r, bx_s, bx_r, bc_s, bc_r,
+           cx_s, cx_r, cc_s, cc_r, l_s, l_r):
+    a = lax.axis_index("aa")
+    b = lax.axis_index("ba")
+    hz, hx = na // 2, nb // 2
+    rank = a * nb + b
+    rows = na * ad
+    cols = na * nb * bd
+    groups = cols // LANES
+    per = LANES // bd
+    mate_a = a + 1 - 2 * lax.rem(a, 2)
+    mate_b = b + 1 - 2 * lax.rem(b, 2)
+
+    def za(base, k):
+        return lax.rem(base + 2 * k, na)
+
+    def zb(base, k):
+        return lax.rem(base + 2 * k, nb)
+
+    barrier = pltpu.get_barrier_semaphore()
+    peers = [(za(a, k), b) for k in range(1, hz)] + [(mate_a, b)]
+    peers += [(a, lax.rem(b + k, nb)) for k in range(1, nb)]
+    for peer in peers:
+        pl.semaphore_signal(barrier, inc=1, device_id=peer, device_id_type=MESH)
+
+    def chosen(index_ref, table_ref):
+        table = table_ref[...]
+        count = index_ref.shape[1]
+        spots = lax.broadcasted_iota(jnp.int32, (table.shape[0], count), 0)
+        hot = jnp.where(spots == index_ref[...], 1.0, 0.0).astype(jnp.bfloat16)
+        return mm(hot, table, TN).astype(jnp.bfloat16)
+
+    a_buf[a] = chosen(ia_ref, ta_ref)
+    own_b = chosen(ib_ref, tb_ref)
+    offset = lax.rem(rank, per) * bd
+    place = (
+        lax.broadcasted_iota(jnp.int32, (bd, LANES), 1)
+        == lax.broadcasted_iota(jnp.int32, (bd, LANES), 0) + offset
+    )
+    placed = mm(
+        jnp.broadcast_to(prior_ref[...].astype(jnp.float32), (PACK, bd)).astype(jnp.bfloat16),
+        jnp.where(place, 1.0, 0.0).astype(jnp.bfloat16),
+    )
+    b_buf[rank, 0:bd] = own_b
+    b_buf[rank, bd:bd + PACK] = placed.astype(jnp.bfloat16)
+    pl.semaphore_wait(barrier, len(peers))
+
+    sent = []
+
+    def send(ref, send_sem, recv_sem, peer):
+        copy = pltpu.make_async_remote_copy(
+            src_ref=ref, dst_ref=ref, send_sem=send_sem, recv_sem=recv_sem,
+            device_id=peer, device_id_type=MESH,
+        )
+        copy.start()
+        sent.append(copy)
+
+    def arrived(ref, send_sem, recv_sem, peer):
+        pltpu.make_async_remote_copy(
+            src_ref=ref, dst_ref=ref, send_sem=send_sem, recv_sem=recv_sem,
+            device_id=peer, device_id_type=MESH,
+        ).wait_recv()
+
+    def spread_b(ref, slot):
+        for k in range(1, hx):
+            where = slot * hx + k
+            send(ref, bx_s.at[where], bx_r.at[where], (a, zb(b, k)))
+        send(ref, bc_s.at[slot * hx], bc_r.at[slot * hx], (a, mate_b))
+
+    own_a_ref = a_buf.at[a]
+    own_b_ref = b_buf.at[rank]
+    for k in range(1, hz):
+        send(own_b_ref, bz_s.at[k], bz_r.at[k], (za(a, k), b))
+    send(own_b_ref, by_s.at[0], by_r.at[0], (mate_a, b))
+    for k in range(1, hz):
+        send(own_a_ref, az_s.at[k], az_r.at[k], (za(a, k), b))
+    spread_b(own_b_ref, 0)
+    send(own_a_ref, ay_s.at[0], ay_r.at[0], (mate_a, b))
+
+    for k in range(1, hz):
+        origin = za(a, hz - k)
+        ref = b_buf.at[origin * nb + b]
+        arrived(ref, bz_s.at[k], bz_r.at[k], (origin, b))
+        send(ref, by_s.at[k], by_r.at[k], (mate_a, b))
+        spread_b(ref, k)
+        ref = a_buf.at[origin]
+        arrived(ref, az_s.at[k], az_r.at[k], (origin, b))
+        send(ref, ay_s.at[k], ay_r.at[k], (mate_a, b))
+    for k in range(hz):
+        origin = za(mate_a, hz - k)
+        ref = b_buf.at[origin * nb + b]
+        arrived(ref, by_s.at[k], by_r.at[k], (mate_a, b))
+        spread_b(ref, hz + k)
+    for k in range(hz):
+        origin = za(mate_a, hz - k)
+        arrived(a_buf.at[origin], ay_s.at[k], ay_r.at[k], (mate_a, b))
+
+    def slot_origin(slot):
+        return za(a, hz - slot) if slot < hz else za(mate_a, 2 * hz - slot)
+
+    for slot in range(na):
+        for k in range(1, hx):
+            where = slot * hx + k
+            from_b = zb(b, hx - k)
+            ref = b_buf.at[slot_origin(slot) * nb + from_b]
+            arrived(ref, bx_s.at[where], bx_r.at[where], (a, from_b))
+            send(ref, bc_s.at[where], bc_r.at[where], (a, mate_b))
+
+    rows_a = a_buf[...].reshape(rows, LANES)
+    factor = SCORE_SCALE * LOG2E
+    query = mm(rows_a, rot_ref[...]) * factor
+    query = jnp.concatenate(pieces(query, 3), axis=1)
+
+    for slot in range(na):
+        for k in range(hx):
+            where = slot * hx + k
+            ref = b_buf.at[slot_origin(slot) * nb + zb(mate_b, hx - k)]
+            arrived(ref, bc_s.at[where], bc_r.at[where], (a, mate_b))
+
+    rows_b = b_buf[:, 0:bd, :].reshape(cols, LANES)
+    rows_b3 = jnp.concatenate([rows_b] * 3, axis=1)
+    for g in range(groups):
+        total = b_buf[g * per, bd:bd + PACK].astype(jnp.float32)
+        for k in range(1, per):
+            total = total + b_buf[g * per + k, bd:bd + PACK].astype(jnp.float32)
+        pb_buf[g:g + 1] = total[0:1] * LOG2E
+
+    def group(g):
+        return slice(g * LANES, (g + 1) * LANES)
+
+    def row_parts(c, pot):
+        here = slice(c * ad, (c + 1) * ad)
+        logits = [s_buf[here, group(g)] + pot[g:g + 1] for g in range(groups)]
+        peak = jnp.max(functools.reduce(jnp.maximum, logits), axis=1, keepdims=True)
+        parts = [jnp.exp2(x - peak) for x in logits]
+        mass = jnp.sum(functools.reduce(jnp.add, parts), axis=1, keepdims=True)
+        return here, peak, parts, mass
+
+    s_buf[...] = mm(query, rows_b3, NT)
+    pot = pb_buf[...]
+    for c in range(na):
+        here, peak, parts, mass = row_parts(c, pot)
+        for g in range(groups):
+            high, low = pieces(parts[g], 2)
+            w_buf[here, group(g)] = high
+            w_buf[here, group(groups + g)] = low
+        pa_buf[here] = jnp.broadcast_to(1.0 / mass, (ad, LANES))
+    mixed = mm(w_buf[...], jnp.concatenate([rows_b, rows_b], axis=0)) * pa_buf[...]
+    both = mm(rows_a, jnp.concatenate(pieces(mixed, 2), axis=1), TN)
+    mine = lax.div(b, 2)
+    cov_buf[mine] = both[:, :LANES] + both[:, LANES:]
+    for k in range(1, hx):
+        send(cov_buf.at[mine], cx_s.at[k], cx_r.at[k], (a, zb(b, k)))
+    for k in range(1, hx):
+        from_b = zb(b, hx - k)
+        arrived(cov_buf.at[lax.div(from_b, 2)], cx_s.at[k], cx_r.at[k], (a, from_b))
+    side = lax.rem(b, 2)
+    cov2_buf[side] = functools.reduce(jnp.add, [cov_buf[k] for k in range(hx)])
+    send(cov2_buf.at[side], cc_s, cc_r, (a, mate_b))
+    arrived(cov2_buf.at[1 - side], cc_s, cc_r, (a, mate_b))
+    current = (cov2_buf[0] + cov2_buf[1]) / (rows * nb)
+    norm = jnp.sum(jnp.sum(current * current, axis=1, keepdims=True), axis=0, keepdims=True)
+    current = current / jnp.sqrt(norm + 1e-06)
+    for sweep in range(NS_ITERS):
+        square = square_product(current, current, 1)
+        current = 1.5 * current - 0.5 * square_product(square, current, 0)
+    rot_out[...] = current
+
+    turn = jnp.concatenate(pieces(current, 3), axis=0)
+    query = mm(jnp.concatenate([rows_a] * 3, axis=1), turn) * factor
+    query = jnp.concatenate(pieces(query, 3), axis=1)
+    s_buf[...] = mm(query, rows_b3, NT)
+
+    for sweep in range(PASSES):
+        for c in range(na):
+            here, peak, parts, mass = row_parts(c, pot)
+            value = -math.log2(rows * nb) - (peak + log2(mass))
+            pa_buf[here] = jnp.broadcast_to(value, (ad, LANES))
+        for g in range(groups):
+            logits = s_buf[:, group(g)] + pa_buf[...]
+            peak = jnp.max(logits, axis=0, keepdims=True)
+            mass = jnp.sum(jnp.exp2(logits - peak), axis=0, keepdims=True)
+            lse_buf[sweep, b, g:g + 1] = peak + log2(mass)
+        for k in range(1, nb):
+            send(lse_buf.at[sweep, b], l_s.at[sweep, k], l_r.at[sweep, k], (a, lax.rem(b + k, nb)))
+        for k in range(1, nb):
+            from_b = lax.rem(b + nb - k, nb)
+            arrived(lse_buf.at[sweep, from_b], l_s.at[sweep, k], l_r.at[sweep, k], (a, from_b))
+        parts = [lse_buf[sweep, k] for k in range(nb)]
+        peak = functools.reduce(jnp.maximum, parts)
+        mass = functools.reduce(jnp.add, [jnp.exp2(x - peak) for x in parts])
+        pot = -math.log2(cols) - (peak + log2(mass))
+
+    def to_row(column, n):
+        eye = (
+            lax.broadcasted_iota(jnp.int32, (n, n), 0)
+            == lax.broadcasted_iota(jnp.int32, (n, n), 1)
+        )
+        return jnp.sum(jnp.where(eye, column, 0.0), axis=0, keepdims=True)
+
+    own = pa_buf[pl.ds(pl.multiple_of(a * ad, 8), ad), 0:ad]
+    pa_out[...] = to_row(own, ad) * LN2
+    pb_buf[...] = pot
+    line = pb_buf[pl.ds(lax.div(rank, per), 1)]
+    column = jnp.sum(
+        jnp.where(place, jnp.broadcast_to(line, (bd, LANES)), 0.0), axis=1, keepdims=True
+    )
+    pb_out[...] = to_row(jnp.broadcast_to(column, (bd, bd)), bd) * LN2
+    for copy in sent:
+        copy.wait_send()
+
+
+def local_kernel(na, nb, table_a, table_b, index_a, index_b, rotation_prev, column_prior):
+    ad, bd = index_a.shape[0], index_b.shape[0]
+    rows, cols = na * ad, na * nb * bd
+    groups = cols // LANES
+    hz, hx = na // 2, nb // 2
+    dma = pltpu.SemaphoreType.DMA
+    f32, bf16 = jnp.float32, jnp.bfloat16
+    rotation, pa, pb = pl.pallas_call(
+        functools.partial(kernel, na, nb, ad, bd),
+        out_shape=(
+            jax.ShapeDtypeStruct((LANES, LANES), f32),
+            jax.ShapeDtypeStruct((1, ad), f32),
+            jax.ShapeDtypeStruct((1, bd), f32),
+        ),
+        in_specs=[pl.BlockSpec(memory_space=pltpu.VMEM)] * 6,
+        out_specs=tuple([pl.BlockSpec(memory_space=pltpu.VMEM)] * 3),
+        scratch_shapes=[
+            pltpu.VMEM((na, ad, LANES), bf16),
+            pltpu.VMEM((na * nb, bd + PACK, LANES), bf16),
+            pltpu.VMEM((rows, cols), f32),
+            pltpu.VMEM((rows, 2 * cols), bf16),
+            pltpu.VMEM((hx, LANES, LANES), f32),
+            pltpu.VMEM((2, LANES, LANES), f32),
+            pltpu.VMEM((PASSES, nb, groups, LANES), f32),
+            pltpu.VMEM((rows, LANES), f32),
+            pltpu.VMEM((groups, LANES), f32),
+            dma((hz,)), dma((hz,)), dma((hz,)), dma((hz,)),
+            dma((hz,)), dma((hz,)), dma((hz,)), dma((hz,)),
+            dma((na * hx,)), dma((na * hx,)), dma((na * hx,)), dma((na * hx,)),
+            dma((hx,)), dma((hx,)), dma, dma,
+            dma((PASSES, nb)), dma((PASSES, nb)),
+        ],
+        compiler_params=pltpu.CompilerParams(collective_id=0, has_side_effects=True),
+    )(
+        table_a, table_b, index_a.reshape(1, ad), index_b.reshape(1, bd),
+        rotation_prev, column_prior.reshape(1, bd),
+    )
+    return rotation, pa.reshape(ad), pb.reshape(bd)
+
+
+def local(table_a, table_b, index_a, index_b, rotation_prev, column_prior):
+    na, nb = lax.axis_size("aa"), lax.axis_size("ba")
+    ad, bd = index_a.shape[0], index_b.shape[0]
+    cols = na * nb * bd
+    fits = (
+        na % 2 == 0 and nb % 2 == 0 and table_a.shape[1] == LANES
+        and ad % PACK == 0 and ad <= LANES and bd % PACK == 0 and LANES % bd == 0
+        and cols % LANES == 0 and 4 * na * ad * cols <= SCORE_BYTES
+    )
+    args = (table_a, table_b, index_a, index_b, rotation_prev, column_prior)
+    return local_kernel(na, nb, *args) if fits else local_collectives(*args)
+
+
 def solution(mesh):
     return jax.shard_map(
         local,

time: 351 us -> 40.7 us (0.12)
  blocking collectives: 191 us -> 0 us
  waiting for transfers between devices: 116 us -> 0 us
  Pallas kernels: 0 us -> 37.3 us
  between operations: 16.4 us -> 0.65 us
  local copies, waits for them, and re-layouts: 13.2 us -> 2.59 us
  other arithmetic: 6.81 us -> 0 us
  matrix products: 6.11 us -> 0 us
    all_gather x8 -> x0, blocking collectives: 141 us -> none  [the longest x6 105 us: combined_all(): everything = jax.tree.map(lambda part: lax.all_gather(part, axis), x)]
    psum x1 -> x0, waiting for transfers between devices: 116 us -> none  [local(): covariance = lax.psum(partial_sum, ('aa', 'ba')) / total_a]
    unnamed x5 -> x0, blocking collectives: 50.6 us -> none
    pallas_call x0 -> x1, Pallas kernels: none -> 37.3 us  [local_kernel(): pl.pallas_call(functools.partial(kernel, na, nb, ad, bd), out_shape=(jax....]
    dot_general x22 -> x0, matrix products: 6.11 us -> none  [the longest x8 2.13 us: polar_factor(): square = jnp.dot(current, current.T, precision=lax.Precision.HIGHEST)]
    unnamed x52 -> x7, local copies, waits for them, and re-layouts: 7.83 us -> 2.59 us
  transfers between devices with their start and end apart: 1 -> 0, of which waited for: 1 -> 0; matrix products, arithmetic and copies ran while one was open for 0% -> 0% of each run, Pallas kernels for 0% -> 0%
where the time goes in v1:
time: 40.7 us; the launch traced here: 40.5 us
  Pallas kernels  37.3 us (92%)
  local copies, waits for them, and re-layouts  2.59 us (6%)
  between operations  0.65 us (2%)
    pallas_call x1, Pallas kernels, local_kernel(): pl.pallas_call(functools.partial(kernel, na, nb, ad, bd), out_shape=(jax....  37.3 us
    unnamed x7, local copies, waits for them, and re-layouts  2.59 us

profile of v1, /device:TPU:0, one launch (start us, length us, event | category | flops | bytes accessed | tf_op | source)
XLA Modules:
  0.0 40.5 jit_solution(3977337305881068146)
XLA Ops:
  0.6 37.3 %shard_map.85 = (f32[128,128]{1,0:T(8,128)}, f32[1,48]{1,0:T(1,128)}, f32[1,32]{1,0:T(1,128)}) custom-call(bf16[192,128]{1,0:T(8,128)(2,1)} %ta_ref.1, bf16[128,128]{1,0:T(8,128)(2,1)} %tb_ref.1, s32[1,48]{1,0:T(1,128)} %bitcast.5, s32[1,32]{1,0:T(1,128)} %bitcast.6, bf16[128,128]{1,0:T(8,128)(2,1)} %rot_ref.1, bf16[1,32]{1,0:T(2,128)(2,1)} %bitcast.7), custom_call_target="tpu_custom_call" | custom-call | tf_op jit(solution)/shard_map/pallas_call | solution.py:367
  37.9 0.0 copy-start.1
  37.9 1.5 %copy.12 = f32[128,128]{1,0:T(8,128)} copy(f32[128,128]{1,0:T(8,128)} %get-tuple-element.12) | data formatting | bytes 131072
  39.4 0.0 copy-done.1
  39.4 0.0 copy-start
  39.4 0.5 %copy.13 = f32[48]{0:T(128)} copy(f32[48]{0:T(128)S(1)} %bitcast.9) | data formatting | bytes 384
  39.9 0.1 copy-done
  40.0 0.5 %copy.14 = f32[32]{0:T(128)} copy(f32[32]{0:T(128)S(1)} %bitcast.8) | data formatting | bytes 256
Async XLA Ops:
  37.9 1.5 %copy-start.1 = (f32[1,48]{1,0:T(1,128)S(1)}, f32[1,48]{1,0:T(1,128)}, u32[]{:S(2)}) copy-start(f32[1,48]{1,0:T(1,128)} %get-tuple-element.7) | copy-start | bytes 580
  39.4 0.6 %copy-start = (f32[1,32]{1,0:T(1,128)S(1)}, f32[1,32]{1,0:T(1,128)}, u32[]{:S(2)}) copy-start(f32[1,32]{1,0:T(1,128)} %get-tuple-element.8) | copy-start | bytes 388

commit v2 on v1

--- a/solution.py
+++ b/solution.py
@@ -142,8 +142,9 @@
 
 
 def kernel(na, nb, ad, bd,
-           ta_ref, tb_ref, ia_ref, ib_ref, rot_ref, prior_ref,
+           ta_in, tb_in, ia_in, ib_in, rot_in, prior_in,
            rot_out, pa_out, pb_out,
+           ta_ref, tb_ref, ia_ref, ib_ref, rot_ref, prior_ref, in_sem,
            a_buf, b_buf, s_buf, w_buf, cov_buf, cov2_buf, lse_buf, pa_buf, pb_buf,
            az_s, az_r, bz_s, bz_r, ay_s, ay_r, by_s, by_r, bx_s, bx_r, bc_s, bc_r,
            cx_s, cx_r, cc_s, cc_r, l_s, l_r):
@@ -170,6 +171,18 @@
     for peer in peers:
         pl.semaphore_signal(barrier, inc=1, device_id=peer, device_id_type=MESH)
 
+    loads = [
+        pltpu.make_async_copy(source, target, in_sem.at[k])
+        for k, (source, target) in enumerate((
+            (ib_in, ib_ref), (tb_in, tb_ref), (prior_in, prior_ref),
+            (ia_in, ia_ref), (ta_in, ta_ref), (rot_in, rot_ref),
+        ))
+    ]
+    for load in loads:
+        load.start()
+    for load in loads:
+        load.wait()
+
     def chosen(index_ref, table_ref):
         table = table_ref[...]
         count = index_ref.shape[1]
@@ -230,6 +243,8 @@
         arrived(ref, bz_s.at[k], bz_r.at[k], (origin, b))
         send(ref, by_s.at[k], by_r.at[k], (mate_a, b))
         spread_b(ref, k)
+    for k in range(1, hz):
+        origin = za(a, hz - k)
         ref = a_buf.at[origin]
         arrived(ref, az_s.at[k], az_r.at[k], (origin, b))
         send(ref, ay_s.at[k], ay_r.at[k], (mate_a, b))
@@ -238,10 +253,6 @@
         ref = b_buf.at[origin * nb + b]
         arrived(ref, by_s.at[k], by_r.at[k], (mate_a, b))
         spread_b(ref, hz + k)
-    for k in range(hz):
-        origin = za(mate_a, hz - k)
-        arrived(a_buf.at[origin], ay_s.at[k], ay_r.at[k], (mate_a, b))
-
     def slot_origin(slot):
         return za(a, hz - slot) if slot < hz else za(mate_a, 2 * hz - slot)
 
@@ -253,6 +264,9 @@
             arrived(ref, bx_s.at[where], bx_r.at[where], (a, from_b))
             send(ref, bc_s.at[where], bc_r.at[where], (a, mate_b))
 
+    for k in range(hz):
+        origin = za(mate_a, hz - k)
+        arrived(a_buf.at[origin], ay_s.at[k], ay_r.at[k], (mate_a, b))
     rows_a = a_buf[...].reshape(rows, LANES)
     factor = SCORE_SCALE * LOG2E
     query = mm(rows_a, rot_ref[...]) * factor
@@ -357,6 +371,12 @@
         copy.wait_send()
 
 
+def finish(rot_ref, pa_ref, pb_ref, rot_out, pa_out, pb_out):
+    rot_out[...] = rot_ref[...]
+    pa_out[...] = pa_ref[...]
+    pb_out[...] = pb_ref[...]
+
+
 def local_kernel(na, nb, table_a, table_b, index_a, index_b, rotation_prev, column_prior):
     ad, bd = index_a.shape[0], index_b.shape[0]
     rows, cols = na * ad, na * nb * bd
@@ -371,9 +391,12 @@
             jax.ShapeDtypeStruct((1, ad), f32),
             jax.ShapeDtypeStruct((1, bd), f32),
         ),
-        in_specs=[pl.BlockSpec(memory_space=pltpu.VMEM)] * 6,
+        in_specs=[pl.BlockSpec(memory_space=pl.ANY)] * 6,
         out_specs=tuple([pl.BlockSpec(memory_space=pltpu.VMEM)] * 3),
         scratch_shapes=[
+            pltpu.VMEM(table_a.shape, bf16), pltpu.VMEM(table_b.shape, bf16),
+            pltpu.VMEM((1, ad), jnp.int32), pltpu.VMEM((1, bd), jnp.int32),
+            pltpu.VMEM((LANES, LANES), bf16), pltpu.VMEM((1, bd), bf16), dma((6,)),
             pltpu.VMEM((na, ad, LANES), bf16),
             pltpu.VMEM((na * nb, bd + PACK, LANES), bf16),
             pltpu.VMEM((rows, cols), f32),
@@ -394,6 +417,16 @@
         table_a, table_b, index_a.reshape(1, ad), index_b.reshape(1, bd),
         rotation_prev, column_prior.reshape(1, bd),
     )
+    rotation, pa, pb = pl.pallas_call(
+        finish,
+        out_shape=(
+            jax.ShapeDtypeStruct((LANES, LANES), f32),
+            jax.ShapeDtypeStruct((1, ad), f32),
+            jax.ShapeDtypeStruct((1, bd), f32),
+        ),
+        in_specs=[pl.BlockSpec(memory_space=pltpu.VMEM)] * 3,
+        out_specs=tuple([pl.BlockSpec(memory_space=pltpu.VMEM)] * 3),
+    )(rotation, pa, pb)
     return rotation, pa.reshape(ad), pb.reshape(bd)
 
 

time: 40.7 us -> 38.7 us (0.951)
  local copies, waits for them, and re-layouts: 2.59 us -> 0 us
  Pallas kernels: 37.3 us -> 37.8 us
    unnamed x7 -> x0, local copies, waits for them, and re-layouts: 2.59 us -> none
    pallas_call x0 -> x1, Pallas kernels: none -> 1.48 us  [local_kernel(): pl.pallas_call(finish, out_shape=(jax.ShapeDtypeStruct((LANES, LANES), f3...]
    pallas_call x1, Pallas kernels: 37.3 us -> 36.3 us  [local_kernel(): pl.pallas_call(functools.partial(kernel, na, nb, ad, bd), out_shape=(jax....]
where the time goes in v2:
time: 38.7 us; the launch traced here: 38.4 us
  Pallas kernels  37.8 us (98%)
  between operations  0.64 us (2%)
    pallas_call x1, Pallas kernels, local_kernel(): pl.pallas_call(functools.partial(kernel, na, nb, ad, bd), out_shape=(jax....  36.3 us
    pallas_call x1, Pallas kernels, local_kernel(): pl.pallas_call(finish, out_shape=(jax.ShapeDtypeStruct((LANES, LANES), f3...  1.48 us

profile of v2, /device:TPU:0, one launch (start us, length us, event | category | flops | bytes accessed | tf_op | source)
XLA Modules:
  0.0 38.4 jit_solution(5869118418819289143)
XLA Ops:
  0.6 36.3 %shard_map.85 = (f32[128,128]{1,0:T(8,128)}, f32[1,48]{1,0:T(1,128)}, f32[1,32]{1,0:T(1,128)}) custom-call(bf16[192,128]{1,0:T(8,128)(2,1)} %ta_in.1, bf16[128,128]{1,0:T(8,128)(2,1)} %tb_in.1, s32[1,48]{1,0:T(1,128)} %bitcast.5, s32[1,32]{1,0:T(1,128)} %bitcast.6, bf16[128,128]{1,0:T(8,128)(2,1)} %rot_in.1, bf16[1,32]{1,0:T(2,128)(2,1)} %bitcast.7), custom_call_target="tpu_custom_call" | custom-call | tf_op jit(solution)/shard_map/pallas_call | solution.py:387
  37.0 1.5 %shard_map.86 = (f32[128,128]{1,0:T(8,128)}, f32[1,48]{1,0:T(1,128)}, f32[1,32]{1,0:T(1,128)}) custom-call(f32[128,128]{1,0:T(8,128)} %get-tuple-element.9.rot_ref, f32[1,48]{1,0:T(1,128)} %get-tuple-element.10.pa_ref, f32[1,32]{1,0:T(1,128)} %get-tuple-element.11.pb_ref), custom_call_target="tpu_custom_call" | custom-call | tf_op jit(solution)/shard_map/pallas_call | solution.py:420
